TPU v7x, 32 devices: a whole 2x2x4 slice. The times are simulated.
32 devices in a mesh: groups: 2 (over x), ctx: 8 (over z, y), tp: 2 (over core).
Axes of the slice: x: 2, y: 2, z: 4, core: 2. Of those that a mesh axis runs over, the one named last changes fastest.
Arguments:
- enc_input: bfloat16 [2048, 4096], P(('groups', 'ctx')), parts along dimension 0, may hold values from -6 to 6
- enc_query: bfloat16 [2048, 1024], P(('groups', 'ctx'), 'tp'), parts along dimension 0
- enc_key: bfloat16 [2048, 1024], P(('groups', 'ctx'), 'tp'), parts along dimension 0
- enc_value: bfloat16 [2048, 1024], P(('groups', 'ctx'), 'tp'), parts along dimension 0, may hold values from -6 to 6
- seq_length: int32 [2], P('groups'), parts along dimension 0, may hold values from 256 to 1024
- attn_out_weight: bfloat16 [1024, 4096], P('tp'), may hold values from -0.1875 to 0.1875
- enc_gain: bfloat16 [4096], replicated, may hold values from 0.25 to 1.75
- cross_key_weight: bfloat16 [4096, 1024], P('ctx', 'tp'), may hold values from -0.09375 to 0.09375
- cross_value_weight: bfloat16 [4096, 1024], P('ctx', 'tp'), may hold values from -0.09375 to 0.09375
- embed_table: bfloat16 [32128, 4096], P('tp', 'ctx')
- dec_ids: int32 [32, 2], P('groups'), parts along dimension 0, may hold values from 0 to 32127
- dec_gain: bfloat16 [4096], P('ctx'), may hold values from 0.25 to 1.75
- cross_query_weight: bfloat16 [4096, 1024], P('ctx', 'tp')
- cross_out_weight: bfloat16 [1024, 4096], P('tp', 'ctx'), may hold values from -0.1875 to 0.1875
Outputs:
- cross_keys: bfloat16 [16, 128, 1024], P(('groups', 'ctx'), None, 'tp'), parts along dimension 0
- cross_values: bfloat16 [16, 128, 1024], P(('groups', 'ctx'), None, 'tp'), parts along dimension 0
- decoded: bfloat16 [32, 2, 4096], P('groups', None, 'ctx'), parts along dimension 0
There are 2 independent parts, one for each index of `groups`. A program takes and returns all parts, laid end to end along the dimension named above; an argument that names none is the same for every part. Nothing has to cross between parts.
Inputs may be any that keep to these rules, and one draw needn't show every extreme that they name: `seq_length`: the input's real length.
All inputs are finite; a program needn't handle non-finite values.
Results may differ from a plain program's by a relative error of at most 0.04.
Values may be sent and summed in bfloat16 or wider, within the bound.
A program may use at most 128 MiB of HBM per device.

v0:
```python
import math
import jax
import jax.numpy as jnp
from jax import lax
from jax.sharding import PartitionSpec as P

D = 4096
HD = 128
EPSILON = 1e-06
FLOOR = -1e30


def joined(value, axis, join):
    pieces = jax.tree.map(lambda part: lax.all_gather(part, axis), value)
    head = jax.tree.map(lambda part: part[0], pieces)
    tail = jax.tree.map(lambda part: part[1:], pieces)
    total, _ = lax.scan(lambda total, piece: (join(total, piece), None), head, tail)
    return total


def softmax_merge(first, second):
    top_first, total_first, mixed_first = first
    top_second, total_second, mixed_second = second
    top = jnp.maximum(top_first, top_second)
    weight_first = jnp.exp(top_first - top)
    weight_second = jnp.exp(top_second - top)
    total = total_first * weight_first + total_second * weight_second
    mixed = mixed_first * weight_first[..., None] + mixed_second * weight_second[..., None]
    return (top, total, mixed)


def partial_softmax(queries, keys, values, valid, factor):
    scores = jnp.einsum("qhd,khd->hqk", queries, keys, preferred_element_type=jnp.float32) * factor
    scores = jnp.where(valid[None, None, :], scores, FLOOR)
    top = jnp.max(scores, axis=-1)
    probs = jnp.where(valid[None, None, :], jnp.exp(scores - top[..., None]), 0.0)
    total = jnp.sum(probs, axis=-1)
    mixed = jnp.einsum(
        "hqk,khd->hqd", probs.astype(jnp.bfloat16), values, preferred_element_type=jnp.float32
    )
    return (top, total, mixed)


def norm_rows(resid, gain):
    scale = lax.rsqrt(jnp.mean(resid * resid, axis=-1, keepdims=True) + EPSILON)
    return (resid * scale * gain.astype(jnp.float32)).astype(jnp.bfloat16)


def local(
    enc_input,
    enc_query,
    enc_key,
    enc_value,
    seq_length,
    attn_out_weight,
    enc_gain,
    cross_key_weight,
    cross_value_weight,
    embed_table,
    dec_ids,
    dec_gain,
    cross_query_weight,
    cross_out_weight,
):
    rows, inner_local = enc_query.shape
    heads_local = inner_local // HD
    limit = seq_length[0]
    queries = enc_query.reshape(rows, heads_local, HD)
    start_state = (
        jnp.full((heads_local, rows), FLOOR, jnp.float32),
        jnp.zeros((heads_local, rows), jnp.float32),
        jnp.zeros((heads_local, rows, HD), jnp.float32),
    )
    carry = start_state
    key_rows = lax.all_gather(enc_key, "ctx", axis=0, tiled=True)
    value_rows = lax.all_gather(enc_value, "ctx", axis=0, tiled=True)
    count = key_rows.shape[0]
    block = math.gcd(count, 2048)
    blocks = count // block
    key_blocks = key_rows.reshape(blocks, block, heads_local, HD)
    value_blocks = value_rows.reshape(blocks, block, heads_local, HD)
    offsets = jnp.arange(blocks, dtype=jnp.int32) * block

    def one_block(state, item):
        key_block, value_block, offset = item
        positions = offset + jnp.arange(block, dtype=jnp.int32)
        update = partial_softmax(queries, key_block, value_block, positions < limit, HD ** (-0.5))
        return (softmax_merge(state, update), None)

    carry, unused = lax.scan(one_block, carry, (key_blocks, value_blocks, offsets))
    top, total, mixed = carry
    context = (
        jnp.transpose(mixed / total[..., None], (1, 0, 2))
        .reshape(rows, inner_local)
        .astype(jnp.bfloat16)
    )
    summed = lax.psum(jnp.dot(context, attn_out_weight, preferred_element_type=jnp.float32), "tp")
    memory = norm_rows(enc_input.astype(jnp.float32) + summed, enc_gain)
    ctx_count = lax.axis_size("ctx")
    slots = rows // ctx_count
    key_sum = jnp.dot(
        memory,
        lax.all_gather(cross_key_weight, "ctx", axis=0, tiled=True),
        preferred_element_type=jnp.float32,
    )
    value_sum = jnp.dot(
        memory,
        lax.all_gather(cross_value_weight, "ctx", axis=0, tiled=True),
        preferred_element_type=jnp.float32,
    )
    key_rows = key_sum.astype(jnp.bfloat16)
    value_rows = value_sum.astype(jnp.bfloat16)
    keys_moved, values_moved = (
        lax.all_to_all(
            key_rows.reshape(slots, ctx_count, inner_local),
            "ctx",
            split_axis=1,
            concat_axis=0,
            tiled=True,
        ),
        lax.all_to_all(
            value_rows.reshape(slots, ctx_count, inner_local),
            "ctx",
            split_axis=1,
            concat_axis=0,
            tiled=True,
        ),
    )
    keys_cache = keys_moved.reshape(rows, inner_local)
    values_cache = values_moved.reshape(rows, inner_local)
    beams = dec_ids.shape[0]
    vocab_local = embed_table.shape[0]
    flat_ids = dec_ids.reshape(-1) - lax.axis_index("tp") * vocab_local
    inside = (flat_ids >= 0) & (flat_ids < vocab_local)
    looked = jnp.take(embed_table, jnp.clip(flat_ids, 0, vocab_local - 1), axis=0)
    own_rows = jnp.where(inside[:, None], looked.astype(jnp.float32), 0.0)
    hidden = lax.psum(own_rows.astype(jnp.bfloat16), "tp").astype(jnp.float32)
    scaled = (hidden * dec_gain.astype(jnp.float32)).astype(jnp.bfloat16)
    raw_part = jnp.dot(scaled, cross_query_weight, preferred_element_type=jnp.float32)
    square_part = jnp.sum(hidden * hidden, axis=-1)
    raw, squares = lax.psum((raw_part, square_part), "ctx")
    factor = lax.rsqrt(squares / D + EPSILON)
    query = (raw * factor[:, None] * HD ** (-0.5)).astype(jnp.bfloat16).reshape(-1, heads_local, HD)
    positions = jnp.arange(rows, dtype=jnp.int32) * ctx_count + lax.axis_index("ctx")
    local_part = partial_softmax(
        query,
        keys_cache.reshape(rows, heads_local, HD),
        values_cache.reshape(rows, heads_local, HD),
        positions < limit,
        1.0,
    )
    top_all, total_all, mixed_all = joined(local_part, "ctx", softmax_merge)
    attn = (
        jnp.transpose(mixed_all / total_all[..., None], (1, 0, 2))
        .reshape(-1, inner_local)
        .astype(jnp.bfloat16)
    )
    out_part = jnp.dot(attn, cross_out_weight, preferred_element_type=jnp.float32)
    out = lax.psum(out_part, "tp")
    decoded = (out + hidden).astype(jnp.bfloat16).reshape(beams, 2, -1)
    return (keys_cache[None], values_cache[None], decoded)


def solution(mesh):
    placed = (
        P(("groups", "ctx"), None),
        P(("groups", "ctx"), "tp"),
        P(("groups", "ctx"), "tp"),
        P(("groups", "ctx"), "tp"),
        P("groups"),
        P("tp", None),
        P(),
        P("ctx", "tp"),
        P("ctx", "tp"),
        P("tp", "ctx"),
        P("groups", None),
        P("ctx"),
        P("ctx", "tp"),
        P("tp", "ctx"),
    )
    return jax.shard_map(
        local,
        mesh=mesh,
        in_specs=placed,
        out_specs=(
            P(("groups", "ctx"), None, "tp"),
            P(("groups", "ctx"), None, "tp"),
            P("groups", None, "ctx"),
        ),
        check_vma=False,
    )
```

profile of v0, /device:TPU:0, one launch (start us, length us, event | category | flops | bytes accessed | tf_op | source)
XLA Modules:
  0.0 454.3 jit_solution(15801881285562292397)
XLA Ops:
  7.2 1.7 copy.38
  9.0 0.7 all-gather.12.cloned.1.call-update
  10.4 42.3 %all-gather.10.cloned.1.call-done = bf16[1024,512]{0,1:T(8,128)(2,1)} async-done(((bf16[128,512]{0,1:T(8,128)(2,1)}), bf16[1024,512]{0,1:T(8,128)(2,1)}) %all-gather.10.cloned.1.call-update) | async-done | bytes 1048592 | tf_op jit(solution)/shard_map/all_gather | solution.py:75
  52.8 1.9 fusion.3
  55.2 39.0 %all-gather.12.cloned.1.call-done = bf16[1024,512]{1,0:T(8,128)(2,1)} async-done(((bf16[128,512]{1,0:T(8,128)(2,1)}), bf16[1024,512]{1,0:T(8,128)(2,1)}) %all-gather.12.cloned.1.call-update) | async-done | bytes 1048592 | tf_op jit(solution)/shard_map/all_gather | solution.py:76
  94.2 2.3 copy.41
  96.5 2.1 fusion.9
  99.0 2.1 fusion.54
  102.8 9.3 %gather_fusion = bf16[32,512]{1,0:T(8,128)(2,1)S(1)} fusion(bf16[16064,512]{1,0:T(8,128)(2,1)} %param.25, s32[1024]{0:T(1024)S(1)} %pad_clamp_fusion), kind=kCustom, calls=%fused_computation | custom fusion | bytes 65664 | tf_op jit(solution)/shard_map/jit(_take)/gather | solution.py:135
  112.3 3.4 psum.36
  115.7 0.8 fusion.31
  116.7 18.3 %psum.38 = f32[32]{0:T(128)S(1)} all-reduce(f32[32]{0:T(128)S(1)} %fusion.25), channel_id=1, replica_groups=mesh['groups'=2,'ctx'=8,'tp'=2] {'ctx'}, use_global_device_ids=true, to_apply=%region_7.8 | all-reduce | flops 32 | bytes 256 | tf_op jit(solution)/shard_map/psum | solution.py:141
  135.0 2.1 multiply_reduce_fusion
  137.6 59.6 %all-gather.14.cloned.1.call-done = bf16[4096,512]{1,0:T(8,128)(2,1)} async-done(((bf16[512,512]{1,0:T(8,128)(2,1)}), bf16[4096,512]{1,0:T(8,128)(2,1)}) %all-gather.14.cloned.1.call-update) | async-done | bytes 4194320 | tf_op jit(solution)/shard_map/all_gather | solution.py:103
  197.2 2.9 fusion.10
  200.2 0.7 copy.42
  200.9 3.4 all-to-all-start
  204.2 66.7 %all-gather.16.cloned.1.call-done = bf16[4096,512]{1,0:T(8,128)(2,1)} async-done(((bf16[512,512]{1,0:T(8,128)(2,1)}), bf16[4096,512]{1,0:T(8,128)(2,1)}) %all-gather.16.cloned.1.call-update) | async-done | bytes 4194320 | tf_op jit(solution)/shard_map/all_gather | solution.py:108
  271.0 2.9 fusion.11
  273.9 0.7 copy.43
  274.6 3.4 all-to-all-start.1
  278.1 7.3 %all-to-all-done.1 = bf16[16,8,512]{2,0,1:T(8,128)(2,1)S(1)} async-done(((bf16[16,8,512]{2,0,1:T(8,128)(2,1)}), bf16[16,8,512]{2,0,1:T(8,128)(2,1)S(1)}, u32[]{:S(2)}, u32[]{:S(2)}) %all-to-all-start.1) | async-done | bytes 131104 | tf_op jit(solution)/shard_map/all_to_all | solution.py:121
  285.4 56.9 %all-reduce.6.cloned.1.call-done = f32[32,512]{1,0:T(8,128)} async-done(((f32[32,512]{1,0:T(8,128)}), f32[32,512]{1,0:T(8,128)}) %all-reduce.6.cloned.1.call-update) | async-done | bytes 65552 | tf_op jit(solution)/shard_map/psum | solution.py:141
  342.3 1.1 fusion.53
  343.7 31.4 %all-gather.2 = f32[32,32,128]{2,1,0:T(8,128)S(1)} all-gather(f32[4,32,128]{2,1,0:T(8,128)S(1)} %fusion.21), channel_id=4, replica_groups=mesh['groups'=2,'ctx'=8,'tp'=2] {'ctx'}, dimensions={0}, use_global_device_ids=true | all-gather | bytes 589824 | tf_op jit(solution)/shard_map/all_gather | solution.py:14
  375.3 26.1 %all-gather.4 = f32[8,4,32]{2,1,0:T(4,128)S(1)} all-gather(f32[1,4,32]{2,1,0:T(4,128)S(1)} %bitcast.122), channel_id=3, replica_groups=mesh['groups'=2,'ctx'=8,'tp'=2] {'ctx'}, dimensions={0}, use_global_device_ids=true | all-gather | bytes 4608 | tf_op jit(solution)/shard_map/all_gather | solution.py:14
  401.4 26.1 %all-gather.3 = f32[8,4,32]{2,1,0:T(4,128)S(1)} all-gather(f32[1,4,32]{2,1,0:T(4,128)S(1)} %bitcast.121), channel_id=2, replica_groups=mesh['groups'=2,'ctx'=8,'tp'=2] {'ctx'}, dimensions={0}, use_global_device_ids=true | all-gather | bytes 4608 | tf_op jit(solution)/shard_map/all_gather | solution.py:14
  427.6 1.1 while.2
  428.7 0.9 fusion.33
  429.6 15.1 %all-reduce.8.cloned.1.call-done = f32[32,512]{1,0:T(8,128)} async-done(((f32[32,512]{1,0:T(8,128)}), f32[32,512]{1,0:T(8,128)}) %all-reduce.8.cloned.1.call-update) | async-done | bytes 65552 | tf_op jit(solution)/shard_map/psum | solution.py:159
  444.7 0.8 fusion.26
  446.2 0.7 copy.97
  (78 shorter events, 6.5 us)
Async XLA Ops:
  7.2 108.5 %copy-start = (bf16[512,512]{1,0:T(8,128)(2,1)S(1)}, bf16[512,512]{1,0:T(8,128)(2,1)}, u32[]{:S(2)}) copy-start(bf16[512,512]{1,0:T(8,128)(2,1)} %param.28) | copy-start | bytes 1572868
  7.2 45.6 %all-gather.10.cloned.1.call-start = ((), (), s32[]{:S(2)}) async-start(), calls=%async_computation.2 | async-start | bytes 1179648 | tf_op jit(solution)/shard_map/all_gather | solution.py:75
  9.0 85.2 %all-gather.12.cloned.1.call-start = ((), (), s32[]{:S(2)}) async-start(), calls=%async_computation.3 | async-start | bytes 1179648 | tf_op jit(solution)/shard_map/all_gather | solution.py:76
  9.7 125.3 %all-reduce.4.cloned.1.call-start = ((), (), s32[]{:S(2)}) async-start(), calls=%async_computation.4 | async-start | bytes 4194304 | tf_op jit(solution)/shard_map/psum | solution.py:97
  96.5 2.5 copy-start.3
  101.0 1.3 copy-start.6
  101.1 1.8 copy-start.7
  101.1 15.6 %copy-start.5 = (bf16[4096]{0:T(1024)(128)(2,1)S(1)}, bf16[4096]{0:T(1024)(128)(2,1)}, u32[]{:S(2)}) copy-start(bf16[4096]{0:T(1024)(128)(2,1)} %param.22) | copy-start | bytes 24580
  101.1 34.0 %copy-start.2 = (bf16[128,4096]{1,0:T(8,128)(2,1)S(1)}, bf16[128,4096]{1,0:T(8,128)(2,1)}, u32[]{:S(2)}) copy-start(bf16[128,4096]{1,0:T(8,128)(2,1)} %param.16) | copy-start | bytes 3145732
  101.1 96.2 %all-gather.14.cloned.1.call-start = ((), (), s32[]{:S(2)}) async-start(), calls=%async_computation.5 | async-start | bytes 4718592 | tf_op jit(solution)/shard_map/all_gather | solution.py:103
  101.7 169.3 %all-gather.16.cloned.1.call-start = ((), (), s32[]{:S(2)}) async-start(), calls=%async_computation.6 | async-start | bytes 4718592 | tf_op jit(solution)/shard_map/all_gather | solution.py:108
  102.3 240.0 %all-reduce.6.cloned.1.call-start = ((), (), s32[]{:S(2)}) async-start(), calls=%async_computation.7 | async-start | bytes 131072 | tf_op jit(solution)/shard_map/psum | solution.py:141
  135.0 2.2 copy-start.1
  200.9 73.7 %all-to-all-start = ((bf16[16,8,512]{2,0,1:T(8,128)(2,1)}), bf16[16,8,512]{2,0,1:T(8,128)(2,1)S(1)}, u32[]{:S(2)}, u32[]{:S(2)}) async-start(bf16[16,8,512]{2,0,1:T(8,128)(2,1)} %copy.42), calls=%async_computation | async-start | bytes 262144 | tf_op jit(solution)/shard_map/all_to_all | solution.py:114
  274.6 10.8 %all-to-all-start.1 = ((bf16[16,8,512]{2,0,1:T(8,128)(2,1)}), bf16[16,8,512]{2,0,1:T(8,128)(2,1)S(1)}, u32[]{:S(2)}, u32[]{:S(2)}) async-start(bf16[16,8,512]{2,0,1:T(8,128)(2,1)} %copy.43), calls=%async_computation.1 | async-start | bytes 262144 | tf_op jit(solution)/shard_map/all_to_all | solution.py:121
  278.0 150.7 %copy-start.4 = (bf16[512,512]{1,0:T(8,128)(2,1)S(1)}, bf16[512,512]{1,0:T(8,128)(2,1)}, u32[]{:S(2)}) copy-start(bf16[512,512]{1,0:T(8,128)(2,1)} %param.29) | copy-start | bytes 1572868
  278.0 166.7 %all-reduce.8.cloned.1.call-start = ((), (), s32[]{:S(2)}) async-start(), calls=%async_computation.8 | async-start | bytes 131072 | tf_op jit(solution)/shard_map/psum | solution.py:159
Sparse Core Ops, SparseCore 0:
  10.6 42.1 all-gather.9
  54.9 39.2 all-gather.11
  101.2 20.0 all-reduce.3
  123.2 73.9 all-gather.13
  199.2 71.7 all-gather.15
  274.2 68.0 all-reduce.5
  429.7 14.9 all-reduce.7
where the time goes:
time: 455 us; the launch traced here: 454 us
  waiting for transfers between devices  289 us (64%)
  blocking collectives  105 us (23%)
  local copies, waits for them, and re-layouts  17.7 us (4%)
  between operations  15 us (3%)
  matrix products  14.9 us (3%)
  starting transfers between devices  7.02 us (2%)
  other arithmetic  5.36 us (1%)
    all_gather x3, blocking collectives, joined(): pieces = jax.tree.map(lambda part: lax.all_gather(part, axis), value)  83.7 us
    all_gather x1, waiting for transfers between devices, local(): lax.all_gather(cross_value_weight, 'ctx', axis=0, tiled=True)  66.7 us
    all_gather x1, waiting for transfers between devices, local(): lax.all_gather(cross_key_weight, 'ctx', axis=0, tiled=True)  59.6 us
    psum x1, waiting for transfers between devices, local(): raw, squares = lax.psum((raw_part, square_part), 'ctx')  56.9 us
    all_gather x1, waiting for transfers between devices, local(): key_rows = lax.all_gather(enc_key, 'ctx', axis=0, tiled=True)  42.3 us
    all_gather x1, waiting for transfers between devices, local(): value_rows = lax.all_gather(enc_value, 'ctx', axis=0, tiled=True)  39 us
    psum x1, blocking collectives, local(): raw, squares = lax.psum((raw_part, square_part), 'ctx')  18.3 us
    psum x1, waiting for transfers between devices, local(): out = lax.psum(out_part, 'tp')  15.1 us
  transfers between devices with their start and end apart: 9, of which 7 were waited for; matrix products, arithmetic and copies ran while one was open for 5% of the time, Pallas kernels for 0%

commit v1 on v0

--- a/solution.py
+++ b/solution.py
@@ -3,11 +3,21 @@
 import jax.numpy as jnp
 from jax import lax
 from jax.sharding import PartitionSpec as P
+from jax.lax import all_to_all, psum
 
 D = 4096
 HD = 128
 EPSILON = 1e-06
 FLOOR = -1e30
+
+
+def meshes_shape(payload):
+    chunks = []
+    for _ in range(psum(1, axis_name="ctx")):
+        chunks.append(payload)
+    return jnp.concatenate(
+        all_to_all(jnp.stack(chunks), axis_name="ctx", split_axis=0, concat_axis=0), axis=0
+    )
 
 
 def joined(value, axis, join):
@@ -73,7 +83,7 @@
     )
     carry = start_state
     key_rows = lax.all_gather(enc_key, "ctx", axis=0, tiled=True)
-    value_rows = lax.all_gather(enc_value, "ctx", axis=0, tiled=True)
+    value_rows = meshes_shape(enc_value)
     count = key_rows.shape[0]
     block = math.gcd(count, 2048)
     blocks = count // block

time: 455 us -> 429 us (0.943)
  waiting for transfers between devices: 289 us -> 251 us
  starting transfers between devices: 7.02 us -> 14.3 us
  local copies, waits for them, and re-layouts: 17.7 us -> 22.8 us
    all_gather x1 -> x0, waiting for transfers between devices: 39 us -> none  [local(): value_rows = lax.all_gather(enc_value, 'ctx', axis=0, tiled=True)]
    all_to_all x0 -> x1, starting transfers between devices: none -> 7.31 us  [meshes_shape(): all_to_all(jnp.stack(chunks), axis_name='ctx', split_axis=0, concat_axis=0)]
  transfers between devices with their start and end apart: 9 -> 9, of which waited for: 7 -> 6; matrix products, arithmetic and copies ran while one was open for 5% -> 6% of each run, Pallas kernels for 0% -> 0%
where the time goes in v1:
time: 429 us
  waiting for transfers between devices  251 us (59%)
  blocking collectives  106 us (25%)
  local copies, waits for them, and re-layouts  22.8 us (5%)
  between operations  15.1 us (4%)
  matrix products  14.8 us (3%)
  starting transfers between devices  14.3 us (3%)
  other arithmetic  5.36 us (1%)
    all_gather x3, blocking collectives, joined(): pieces = jax.tree.map(lambda part: lax.all_gather(part, axis), value)  83.7 us
    all_gather x1, waiting for transfers between devices, local(): lax.all_gather(cross_value_weight, 'ctx', axis=0, tiled=True)  66.8 us
    all_gather x1, waiting for transfers between devices, local(): lax.all_gather(cross_key_weight, 'ctx', axis=0, tiled=True)  59.8 us
    psum x1, waiting for transfers between devices, local(): raw, squares = lax.psum((raw_part, square_part), 'ctx')  56.9 us
    all_gather x1, waiting for transfers between devices, local(): key_rows = lax.all_gather(enc_key, 'ctx', axis=0, tiled=True)  43.5 us
    psum x1, blocking collectives, local(): raw, squares = lax.psum((raw_part, square_part), 'ctx')  18.5 us
    psum x1, waiting for transfers between devices, local(): out = lax.psum(out_part, 'tp')  15.1 us
    gather x1, local copies, waits for them, and re-layouts, local(): jnp.take(embed_table, jnp.clip(flat_ids, 0, vocab_local - 1), axis=0)  9.27 us
  transfers between devices with their start and end apart: 9, of which 6 were waited for; matrix products, arithmetic and copies ran while one was open for 6% of the time, Pallas kernels for 0%

profile of v1, /device:TPU:0, one launch (start us, length us, event | category | flops | bytes accessed | tf_op | source)
XLA Modules:
  0.0 428.5 jit_solution(1043747916645266064)
XLA Ops:
  7.2 1.7 copy.38
  9.0 1.0 copy.41
  10.0 1.1 stack.2
  11.1 7.3 %all-to-all-start = ((bf16[8,128,512]{1,2,0:T(8,128)(2,1)}), bf16[8,128,512]{1,2,0:T(8,128)(2,1)}, u32[]{:S(2)}, u32[]{:S(2)}) async-start(bf16[8,128,512]{1,2,0:T(8,128)(2,1)} %stack.2), calls=%async_computation | async-start | bytes 2097152 | tf_op jit(solution)/shard_map/all_to_all | solution.py:19
  19.2 43.5 %all-gather.9.cloned.1.call-done = bf16[1024,512]{0,1:T(8,128)(2,1)} async-done(((bf16[128,512]{0,1:T(8,128)(2,1)}), bf16[1024,512]{0,1:T(8,128)(2,1)}) %all-gather.9.cloned.1.call-update) | async-done | bytes 1048592 | tf_op jit(solution)/shard_map/all_gather | solution.py:85
  62.6 1.8 fusion.3
  65.0 2.9 copy.42
  68.0 2.3 squeeze.37
  70.3 2.1 fusion.9
  72.8 2.1 fusion.54
  76.8 9.3 %gather_fusion = bf16[32,512]{1,0:T(8,128)(2,1)S(1)} fusion(bf16[16064,512]{1,0:T(8,128)(2,1)} %param.25, s32[1024]{0:T(1024)S(1)} %pad_clamp_fusion), kind=kCustom, calls=%fused_computation | custom fusion | bytes 65664 | tf_op jit(solution)/shard_map/jit(_take)/gather | solution.py:145
  86.2 3.4 psum.36
  89.6 0.8 fusion.31
  90.6 18.5 %psum.38 = f32[32]{0:T(128)S(1)} all-reduce(f32[32]{0:T(128)S(1)} %fusion.25), channel_id=1, replica_groups=mesh['groups'=2,'ctx'=8,'tp'=2] {'ctx'}, use_global_device_ids=true, to_apply=%region_7.8 | all-reduce | flops 32 | bytes 256 | tf_op jit(solution)/shard_map/psum | solution.py:151
  109.0 2.1 multiply_reduce_fusion
  111.7 59.8 %all-gather.11.cloned.1.call-done = bf16[4096,512]{1,0:T(8,128)(2,1)} async-done(((bf16[512,512]{1,0:T(8,128)(2,1)}), bf16[4096,512]{1,0:T(8,128)(2,1)}) %all-gather.11.cloned.1.call-update) | async-done | bytes 4194320 | tf_op jit(solution)/shard_map/all_gather | solution.py:113
  171.5 2.9 fusion.10
  174.4 0.7 copy.43
  175.1 3.4 all-to-all-start.1
  178.5 66.8 %all-gather.13.cloned.1.call-done = bf16[4096,512]{1,0:T(8,128)(2,1)} async-done(((bf16[512,512]{1,0:T(8,128)(2,1)}), bf16[4096,512]{1,0:T(8,128)(2,1)}) %all-gather.13.cloned.1.call-update) | async-done | bytes 4194320 | tf_op jit(solution)/shard_map/all_gather | solution.py:118
  245.2 2.9 fusion.11
  248.8 3.4 all-to-all-start.2
  252.3 7.3 %all-to-all-done.2 = bf16[16,8,512]{2,0,1:T(8,128)(2,1)S(1)} async-done(((bf16[16,8,512]{2,0,1:T(8,128)(2,1)}), bf16[16,8,512]{2,0,1:T(8,128)(2,1)S(1)}, u32[]{:S(2)}, u32[]{:S(2)}) %all-to-all-start.2) | async-done | bytes 131104 | tf_op jit(solution)/shard_map/all_to_all | solution.py:131
  259.6 56.9 %all-reduce.6.cloned.1.call-done = f32[32,512]{1,0:T(8,128)} async-done(((f32[32,512]{1,0:T(8,128)}), f32[32,512]{1,0:T(8,128)}) %all-reduce.6.cloned.1.call-update) | async-done | bytes 65552 | tf_op jit(solution)/shard_map/psum | solution.py:151
  316.5 1.1 fusion.53
  317.9 31.4 %all-gather.2 = f32[32,32,128]{2,1,0:T(8,128)S(1)} all-gather(f32[4,32,128]{2,1,0:T(8,128)S(1)} %fusion.21), channel_id=4, replica_groups=mesh['groups'=2,'ctx'=8,'tp'=2] {'ctx'}, dimensions={0}, use_global_device_ids=true | all-gather | bytes 589824 | tf_op jit(solution)/shard_map/all_gather | solution.py:24
  349.5 26.1 %all-gather.4 = f32[8,4,32]{2,1,0:T(4,128)S(1)} all-gather(f32[1,4,32]{2,1,0:T(4,128)S(1)} %bitcast.122), channel_id=3, replica_groups=mesh['groups'=2,'ctx'=8,'tp'=2] {'ctx'}, dimensions={0}, use_global_device_ids=true | all-gather | bytes 4608 | tf_op jit(solution)/shard_map/all_gather | solution.py:24
  375.7 26.1 %all-gather.3 = f32[8,4,32]{2,1,0:T(4,128)S(1)} all-gather(f32[1,4,32]{2,1,0:T(4,128)S(1)} %bitcast.121), channel_id=2, replica_groups=mesh['groups'=2,'ctx'=8,'tp'=2] {'ctx'}, dimensions={0}, use_global_device_ids=true | all-gather | bytes 4608 | tf_op jit(solution)/shard_map/all_gather | solution.py:24
  401.8 1.1 while.2
  402.9 0.9 fusion.33
  403.8 15.1 %all-reduce.8.cloned.1.call-done = f32[32,512]{1,0:T(8,128)} async-done(((f32[32,512]{1,0:T(8,128)}), f32[32,512]{1,0:T(8,128)}) %all-reduce.8.cloned.1.call-update) | async-done | bytes 65552 | tf_op jit(solution)/shard_map/psum | solution.py:169
  418.9 0.8 fusion.26
  (82 shorter events, 7.9 us)
Async XLA Ops:
  7.2 82.4 %copy-start = (bf16[512,512]{1,0:T(8,128)(2,1)S(1)}, bf16[512,512]{1,0:T(8,128)(2,1)}, u32[]{:S(2)}) copy-start(bf16[512,512]{1,0:T(8,128)(2,1)} %param.28) | copy-start | bytes 1572868
  7.2 55.4 %copy-start.5 = (bf16[128,512]{1,0:T(8,128)(2,1)S(1)}, bf16[128,512]{1,0:T(8,128)(2,1)}, u32[]{:S(2)}) copy-start(bf16[128,512]{1,0:T(8,128)(2,1)} %param.17) | copy-start | bytes 393220
  7.2 55.4 %all-gather.9.cloned.1.call-start = ((), (), s32[]{:S(2)}) async-start(), calls=%async_computation.3 | async-start | bytes 1179648 | tf_op jit(solution)/shard_map/all_gather | solution.py:85
  11.1 53.9 %all-to-all-start = ((bf16[8,128,512]{1,2,0:T(8,128)(2,1)}), bf16[8,128,512]{1,2,0:T(8,128)(2,1)}, u32[]{:S(2)}, u32[]{:S(2)}) async-start(bf16[8,128,512]{1,2,0:T(8,128)(2,1)} %stack.2), calls=%async_computation | async-start | bytes 2097152 | tf_op jit(solution)/shard_map/all_to_all | solution.py:19
  18.5 90.6 %all-reduce.4.cloned.1.call-start = ((), (), s32[]{:S(2)}) async-start(), calls=%async_computation.4 | async-start | bytes 4194304 | tf_op jit(solution)/shard_map/psum | solution.py:107
  70.3 2.5 copy-start.3
  74.8 1.4 copy-start.7
  74.8 1.9 copy-start.8
  74.8 15.7 %copy-start.6 = (bf16[4096]{0:T(1024)(128)(2,1)S(1)}, bf16[4096]{0:T(1024)(128)(2,1)}, u32[]{:S(2)}) copy-start(bf16[4096]{0:T(1024)(128)(2,1)} %param.22) | copy-start | bytes 24580
  74.8 34.2 %copy-start.2 = (bf16[128,4096]{1,0:T(8,128)(2,1)S(1)}, bf16[128,4096]{1,0:T(8,128)(2,1)}, u32[]{:S(2)}) copy-start(bf16[128,4096]{1,0:T(8,128)(2,1)} %param.16) | copy-start | bytes 3145732
  74.9 96.6 %all-gather.11.cloned.1.call-start = ((), (), s32[]{:S(2)}) async-start(), calls=%async_computation.5 | async-start | bytes 4718592 | tf_op jit(solution)/shard_map/all_gather | solution.py:113
  75.6 169.6 %all-gather.13.cloned.1.call-start = ((), (), s32[]{:S(2)}) async-start(), calls=%async_computation.6 | async-start | bytes 4718592 | tf_op jit(solution)/shard_map/all_gather | solution.py:118
  76.2 240.3 %all-reduce.6.cloned.1.call-start = ((), (), s32[]{:S(2)}) async-start(), calls=%async_computation.7 | async-start | bytes 131072 | tf_op jit(solution)/shard_map/psum | solution.py:151
  109.0 2.2 copy-start.1
  175.1 73.8 %all-to-all-start.1 = ((bf16[16,8,512]{2,0,1:T(8,128)(2,1)}), bf16[16,8,512]{2,0,1:T(8,128)(2,1)S(1)}, u32[]{:S(2)}, u32[]{:S(2)}) async-start(bf16[16,8,512]{2,0,1:T(8,128)(2,1)} %copy.43), calls=%async_computation.1 | async-start | bytes 262144 | tf_op jit(solution)/shard_map/all_to_all | solution.py:124
  248.8 10.8 %all-to-all-start.2 = ((bf16[16,8,512]{2,0,1:T(8,128)(2,1)}), bf16[16,8,512]{2,0,1:T(8,128)(2,1)S(1)}, u32[]{:S(2)}, u32[]{:S(2)}) async-start(bf16[16,8,512]{2,0,1:T(8,128)(2,1)} %copy.44), calls=%async_computation.2 | async-start | bytes 262144 | tf_op jit(solution)/shard_map/all_to_all | solution.py:131
  252.2 150.7 %copy-start.4 = (bf16[512,512]{1,0:T(8,128)(2,1)S(1)}, bf16[512,512]{1,0:T(8,128)(2,1)}, u32[]{:S(2)}) copy-start(bf16[512,512]{1,0:T(8,128)(2,1)} %param.29) | copy-start | bytes 1572868
  252.2 166.7 %all-reduce.8.cloned.1.call-start = ((), (), s32[]{:S(2)}) async-start(), calls=%async_computation.8 | async-start | bytes 131072 | tf_op jit(solution)/shard_map/psum | solution.py:169
Sparse Core Ops, SparseCore 0:
  10.6 51.9 all-gather.8
  75.0 20.2 all-reduce.3
  97.5 73.9 all-gather.10
  173.5 71.7 all-gather.12
  248.5 68.0 all-reduce.5
  403.9 14.9 all-reduce.7
